TPU v7x, 32 devices: a whole 2x2x4 slice. The times are simulated.
32 devices in a mesh: inv: 2 (over y), test: 2 (over core), tx: 4 (over z), ty: 2 (over x).
Axes of the slice: x: 2, y: 2, z: 4, core: 2. Of those that a mesh axis runs over, the one named last changes fastest.
Arguments:
- log_cond: float32 [2560, 512], P(('inv', 'tx'), 'ty'), parts along dimension 0, may hold values from -3.5 to -1.7
- log_shape: float32 [2560, 512], P(('inv', 'tx'), 'ty'), parts along dimension 0, may hold values from -2.8 to -1.6
- zone_ids: int32 [2560, 512], P(('inv', 'tx'), 'ty'), parts along dimension 0, may hold values from 0 to 7
- storage: float32 [4, 8], P('inv'), parts along dimension 0, may hold values from 0.9 to 1.2
- pump_x: int32 [4, 1], P(('inv', 'test')), parts along dimension 0, may hold values from 0 to 1279
- pump_y: int32 [4, 1], P(('inv', 'test')), parts along dimension 0, may hold values from 0 to 511
- pump_rates: float32 [4, 3, 1], P(('inv', 'test')), parts along dimension 0, may hold values from -4 to -1
- obs_x: int32 [128], P('inv'), parts along dimension 0, may hold values from 0 to 1279
- obs_y: int32 [128], P('inv'), parts along dimension 0, may hold values from 0 to 511
- observed: float32 [4, 3, 64], P(('inv', 'test')), parts along dimension 0, may hold values from -6 to 6
- frac_start: float32 [4, 1280, 512], P(('inv', 'test'), 'tx', 'ty'), parts along dimension 0, may hold values from -6 to 6
- matrix_start: float32 [4, 1280, 512], P(('inv', 'test'), 'tx', 'ty'), parts along dimension 0, may hold values from -6 to 6
- frac_end: float32 [4, 1280, 512], P(('inv', 'test'), 'tx', 'ty'), parts along dimension 0, may hold values from -6 to 6
- matrix_end: float32 [4, 1280, 512], P(('inv', 'test'), 'tx', 'ty'), parts along dimension 0, may hold values from -6 to 6
Outputs:
- cond_direction: float32 [2560, 512], P(('inv', 'tx'), 'ty'), parts along dimension 0
- shape_direction: float32 [2560, 512], P(('inv', 'tx'), 'ty'), parts along dimension 0
- frac_adjoint: float32 [4, 1280, 512], P(('inv', 'test'), 'tx', 'ty'), parts along dimension 0
- matrix_adjoint: float32 [4, 1280, 512], P(('inv', 'test'), 'tx', 'ty'), parts along dimension 0
There are 2 independent parts, one for each index of `inv`. A program takes and returns all parts, laid end to end along the dimension named above; each array names one. Nothing has to cross between parts.
All inputs are finite; a program needn't handle non-finite values.
Results may differ from a plain program's by a relative error of at most 0.0001.
Values sent between devices are 32-bit elements; how exact they have to be, the bound alone decides.
No kernel may reach another device: no remote copies, remote signals or barrier semaphores. Data moves between devices by JAX's collectives and lax.ppermute only.
A program may use at most 64 MiB of HBM per device.

v0:
```python
import jax
import jax.numpy as jnp
from jax import lax
from jax.sharding import PartitionSpec as P

SMOOTH = 2
blend_rate = 0.2


def padded_2(cells, sides, width):
    for axis, dim in sides:
        count = lax.axis_size(axis)
        ends = count - 1
        head = lax.slice_in_dim(cells, 0, width, axis=dim)
        tail = lax.slice_in_dim(cells, cells.shape[dim] - width, cells.shape[dim], axis=dim)
        cells = jnp.concatenate(
            [
                lax.ppermute(tail, axis, [(i, (i + 1) % count) for i in range(ends)]),
                cells,
                lax.ppermute(head, axis, [((i + 1) % count, i) for i in range(ends)]),
            ],
            axis=dim,
        )
    return cells


def neighbours(padded):
    return (
        padded[..., :-2, 1:-1],
        padded[..., 2:, 1:-1],
        padded[..., 1:-1, :-2],
        padded[..., 1:-1, 2:],
    )


def flow_sum(padded, conductances):
    centre = padded[..., 1:-1, 1:-1]
    summed = jnp.zeros_like(centre)
    for conductance, beside in zip(conductances, neighbours(padded)):
        summed = summed + conductance * (beside - centre)
    return summed


def zero_border(field):
    return jnp.pad(field, [(0, 0)] * (field.ndim - 2) + [(1, 1), (1, 1)])


def local_spots(coord_x, coord_y, tile_rows, tile_cols, margin):
    local_x = coord_x - lax.axis_index("tx") * tile_rows + margin
    local_y = coord_y - lax.axis_index("ty") * tile_cols + margin
    extent_x = tile_rows + 2 * margin
    extent_y = tile_cols + 2 * margin
    inside = (local_x >= 0) & (local_x < extent_x) & (local_y >= 0) & (local_y < extent_y)
    return (jnp.clip(local_x, 0, extent_x - 1), jnp.clip(local_y, 0, extent_y - 1), inside)


def smooth(grad_field):
    for sweep_index in range(SMOOTH):
        padded = padded_2(grad_field, (("tx", 1), ("ty", 2)), 1)
        nearby = neighbours(padded)
        grad_field = grad_field + blend_rate * (
            nearby[0] + nearby[1] + nearby[2] + nearby[3] - 4.0 * grad_field
        )
    return grad_field


def margin_window(
    cond,
    shape_factor,
    store_frac,
    store_matrix,
    pump_x,
    pump_y,
    pump_rates,
    obs_x,
    obs_y,
    observed,
    frac_start,
    matrix_start,
    frac_end,
    matrix_end,
):
    tile_rows, tile_cols = cond.shape
    test_count = frac_start.shape[0]
    step_count = pump_rates.shape[1]
    margin = 2 * step_count
    packed = jnp.concatenate(
        [
            cond[None],
            shape_factor[None],
            store_frac[None],
            store_matrix[None],
            frac_start,
            matrix_start,
            frac_end,
            matrix_end,
        ],
        0,
    )
    widened = padded_2(packed, (("tx", 1), ("ty", 2)), margin)
    place_x = lax.axis_index("tx") * tile_rows - margin + jnp.arange(tile_rows + 2 * margin)
    place_y = lax.axis_index("ty") * tile_cols - margin + jnp.arange(tile_cols + 2 * margin)
    within = ((place_x >= 0) & (place_x < tile_rows * lax.axis_size("tx")))[:, None] & (
        (place_y >= 0) & (place_y < tile_cols * lax.axis_size("ty"))
    )[None, :]
    cond_wide = widened[0]
    shape_wide = widened[1]
    sfrac_wide = jnp.where(within, widened[2], 1.0)
    smatrix_wide = jnp.where(within, widened[3], 1.0)
    fracture = widened[4 : 4 + test_count]
    matrix = widened[4 + test_count : 4 + 2 * test_count]
    end_frac = widened[4 + 2 * test_count : 4 + 3 * test_count]
    end_matrix = widened[4 + 3 * test_count : 4 + 4 * test_count]
    cond_nearby = neighbours(zero_border(cond_wide))
    conductances = []
    slopes = []
    for beside in cond_nearby:
        total = cond_wide + beside
        safe_total = jnp.where(total > 0.0, total, 1.0)
        conductances.append(2.0 * cond_wide * beside / safe_total)
        slopes.append(2.0 * beside * beside / (safe_total * safe_total))
    spot_x, spot_y, spot_in = local_spots(pump_x, pump_y, tile_rows, tile_cols, margin)
    test_rows = jnp.arange(test_count)[:, None]
    obs_lx, obs_ly, obs_in = local_spots(obs_x, obs_y, tile_rows, tile_cols, margin)
    stored = []
    mismatches = []
    for step_index in range(step_count):
        stored.append((fracture, matrix))
        transfer = shape_wide * (fracture - matrix)
        source = (
            jnp.zeros_like(fracture)
            .at[test_rows, spot_x, spot_y]
            .add(jnp.where(spot_in, pump_rates[:, step_index], 0.0))
        )
        fracture_next = (
            fracture
            + (flow_sum(zero_border(fracture), conductances) - transfer + source) / sfrac_wide
        )
        matrix = matrix + transfer / smatrix_wide
        fracture = fracture_next
        mismatches.append(
            jnp.where(obs_in[None], fracture[:, obs_lx, obs_ly] - observed[:, step_index], 0.0)
        )

    def inject(adjoint_field, mismatch):
        return adjoint_field.at[:, obs_lx, obs_ly].add(mismatch)

    def interior(field):
        return field[..., margin : margin + tile_rows, margin : margin + tile_cols]

    fracture_adj = inject(end_frac, mismatches[step_count - 1])
    matrix_adj = end_matrix
    grad_cond = jnp.zeros((tile_rows, tile_cols), jnp.float32)
    grad_shape = jnp.zeros((tile_rows, tile_cols), jnp.float32)
    for step_index in reversed(range(step_count)):
        fracture, matrix = stored[step_index]
        scaled = fracture_adj / sfrac_wide
        matrix_scaled = matrix_adj / smatrix_wide
        scaled_pad = zero_border(scaled)
        spread = flow_sum(scaled_pad, conductances)
        face_term = jnp.zeros_like(fracture)
        for slope, head_beside, adjoint_beside in zip(
            slopes, neighbours(zero_border(fracture)), neighbours(scaled_pad)
        ):
            face_term = face_term + slope * (head_beside - fracture) * (scaled - adjoint_beside)
        grad_cond = grad_cond + interior(cond_wide * jnp.sum(face_term, axis=0))
        swap_rate = shape_wide * (matrix_scaled - scaled)
        grad_shape = grad_shape + interior(jnp.sum(swap_rate * (fracture - matrix), axis=0))
        fracture_adj = fracture_adj + spread + swap_rate
        matrix_adj = matrix_adj - swap_rate
        if step_index > 0:
            fracture_adj = inject(fracture_adj, mismatches[step_index - 1])
    return (grad_cond, grad_shape, interior(fracture_adj), interior(matrix_adj))


def on_device(
    log_cond,
    log_shape,
    zone_ids,
    storage,
    pump_x,
    pump_y,
    pump_rates,
    obs_x,
    obs_y,
    observed,
    frac_start,
    matrix_start,
    frac_end,
    matrix_end,
):
    cond = jnp.exp(log_cond)
    shape_factor = jnp.exp(log_shape)
    store_frac = jnp.zeros_like(cond)
    store_matrix = jnp.zeros_like(cond)
    for zone_index in range(storage.shape[1]):
        chosen = zone_ids == zone_index
        store_frac = jnp.where(chosen, storage[0, zone_index], store_frac)
        store_matrix = jnp.where(chosen, storage[1, zone_index], store_matrix)
    grad_cond, grad_shape, fracture_adj, matrix_adj = margin_window(
        cond,
        shape_factor,
        store_frac,
        store_matrix,
        pump_x,
        pump_y,
        pump_rates,
        obs_x,
        obs_y,
        observed,
        frac_start,
        matrix_start,
        frac_end,
        matrix_end,
    )
    stacked = jnp.stack([grad_cond, grad_shape], 0)
    summed = lax.psum(stacked, "test")
    smoothed = smooth(summed)
    return (smoothed[0], smoothed[1], fracture_adj, matrix_adj)


def solution(mesh):
    placed = (
        P(("inv", "tx"), "ty"),
        P(("inv", "tx"), "ty"),
        P(("inv", "tx"), "ty"),
        P("inv", None),
        P(("inv", "test"), None),
        P(("inv", "test"), None),
        P(("inv", "test"), None, None),
        P("inv"),
        P("inv"),
        P(("inv", "test"), None, None),
        P(("inv", "test"), "tx", "ty"),
        P(("inv", "test"), "tx", "ty"),
        P(("inv", "test"), "tx", "ty"),
        P(("inv", "test"), "tx", "ty"),
    )
    return jax.shard_map(
        on_device,
        mesh=mesh,
        in_specs=placed,
        out_specs=(
            P(("inv", "tx"), "ty"),
            P(("inv", "tx"), "ty"),
            P(("inv", "test"), "tx", "ty"),
            P(("inv", "test"), "tx", "ty"),
        ),
        check_vma=False,
    )
```

profile of v0, /device:TPU:0, one launch (start us, length us, event | category | flops | bytes accessed | tf_op | source)
XLA Modules:
  0.0 218.5 jit_solution(2237124378234032437)
XLA Ops:
  7.2 2.0 fusion.52
  9.2 1.9 copy.72
  11.1 1.9 copy.73
  13.0 1.9 copy.74
  14.9 1.9 copy.82
  16.8 1.9 copy.83
  22.0 6.5 %bitcast_dynamic-update-slice_fusion.1 = (f32[8,320,256]{1,2,0:T(8,128)S(1)}, pred[320,256]{0,1:T(8,128)(4,1)S(1)}, pred[320,256]{0,1:T(8,128)(4,1)S(1)}, pred[3...) fusion(f32[8,320,256]{1,2,0:T(8,128)S(1)} %bitcast_dynamic-upda, ...), kind=kLoop, calls=%fused_computation.121 | loop fusion | flops 1310720 | bytes 1507360
  28.5 5.3 %bitcast_dynamic-update-slice_fusion = f32[8,320,256]{1,2,0:T(8,128)S(1)} fusion(f32[8,320,256]{1,2,0:T(8,128)S(1)} %get-tuple-element.72, pred[320,256]{0,1:T(8,128)(4,1)S(1)} %get-tuple-element.80, pred[320,256]{0,1:T(8,128)(4,1)S(1)} %get-tuple-element.79, pred[320,256]{0,1:T(8,128)(4,1)S(1)} %get-tuple-element.78, ...), kind=kLoop, calls=%fused_computation.120 | loop fusion | flops 655360 | bytes 1179680
  34.1 1.9 fusion.49
  36.0 1.5 copy.87
  38.9 1.6 copy.86
  40.4 5.6 %collective-permute-start = (f32[8,6,256]{2,0,1:T(8,128)S(1)}, f32[8,6,256]{2,0,1:T(8,128)S(1)}, u32[]{:S(2)}, u32[]{:S(2)}) collective-permute-start(f32[8,6,256]{2,0,1:T(8,128)S(1)} %copy.86), channel_id=1, source_target_pairs={{0,2},{2,4},{4,6},{1,3},{3,5},{5,7},{8,10},{10,12},{12,14},{9,11},... | collective-permute-start | bytes 147464 | tf_op jit(solution)/shard_map/ppermute | solution.py:18
  52.8 1.4 copy.88
  56.6 3.8 %collective-permute-start.2 = (f32[8,332,6]{1,2,0:T(8,128)S(1)}, f32[8,332,6]{1,2,0:T(8,128)S(1)}, u32[]{:S(2)}, u32[]{:S(2)}) collective-permute-start(f32[8,332,6]{1,2,0:T(8,128)S(1)} %get-tuple-element.81), channel_id=1, source_target_pairs={{0,1},{2,3},{4,5},{6,7},{8,9},{10,11},{12,13},{14,15},{16,17},{18,... | collective-permute-start | bytes 191240 | tf_op jit(solution)/shard_map/ppermute | solution.py:18
  62.6 4.3 %collective-permute-done.3 = f32[8,332,6]{1,2,0:T(8,128)S(1)} collective-permute-done((f32[8,332,6]{1,2,0:T(8,128)S(1)}, f32[8,332,6]{1,2,0:T(8,128)S(1)}, u32[]{:S(2)}, u32[]{:S(2)}) %collective-permute-start.3) | collective-permute-done | bytes 63776 | tf_op jit(solution)/shard_map/ppermute | solution.py:20
  66.9 3.2 %pad_maximum_fusion = f32[8,332,268]{1,2,0:T(8,128)S(1)} fusion(f32[8,332,6]{1,2,0:T(8,128)S(1)} %collective-permute-done.3, f32[8,6,256]{1,2,0:T(8,128)S(1)} %copy-done.17, f32[8,320,256]{1,2,0:T(8,128)} %copy-done, f32[8,6,256]{1,2,0:T(8,128)S(1)} %copy-done.16, f32[8,332,6]{1,2,0:T(8,128)S(1)} %collective-permute-done.2), kind=kLoop, calls=%fused_computation.6 | loop fusion | flops 2847232 | bytes 5694464 | tf_op jit(solution)/shard_map/concatenate | solution.py:16
  71.0 1.9 add_subtract_fusion.2
  75.0 1.4 add.283
  78.3 2.8 %add_subtract_fusion.1 = (f32[1,332,268]{1,2,0:T(8,128)S(1)}, f32[1,332,268]{1,2,0:T(8,128)}, f32[1,332,268]{1,2,0:T(8,128)}) fusion(f32[1,332,268]{1,2,0:T(8,128)} %get-tuple-element.71, f32[1,332,268]{1,2,0:T(8,128)} %get-tuple-element.70, f32[1,332,268]{1,2,0:T(8,128)} %get-tuple-element.69, f32[1,332,268]{1,2,0:T(8,128)} %get-tuple-element.68, ...), kind=kLoop, calls=%fused_computation.82 | loop fusion | flops 1779520 | bytes 4271448 | tf_op jit(solution)/shard_map/sub | solution.py:137
  82.5 2.0 add.294
  84.5 2.0 divide_add_fusion
  86.5 1.9 gather_fusion.2
  88.4 1.9 gather_fusion.1
  90.3 2.7 %multiply_subtract_fusion = f32[1,332,268]{1,2,0:T(8,128)S(1)} fusion(f32[1,332,268]{1,2,0:T(8,128)} %get-tuple-element.71, f32[1,332,268]{1,2,0:T(8,128)} %get-tuple-element.70, f32[1,332,268]{1,2,0:T(8,128)} %get-tuple-element.69, f32[1,332,268]{1,2,0:T(8,128)} %get-tuple-element.68, f32[8,332,268]{1,2,0:T(8,128)S(1)} %pad_maximum_fusion, ...), kind=kLoop, calls=%fused_computation.74 | loop fusion | flops 1690544 | bytes 3559640 | tf_op jit(solution)/shard_map/sub | solution.py:137
  94.4 2.0 add.305
  96.4 2.2 add_bitcast_fusion.3
  98.6 1.9 gather_fusion
  100.5 9.1 %scatter_fusion = f32[332,268]{0,1:T(8,128)} fusion(f32[332,268]{0,1:T(8,128)} %get-tuple-element.84, s32[64]{0:T(128)S(1)} %get-tuple-element.110, f32[64]{0:T(128)S(1)} %get-tuple-element.108), kind=kCustom, calls=%fused_computation.3 | custom fusion | flops 64 | bytes 1280 | tf_op jit(solution)/shard_map/scatter-add | solution.py:146
  109.6 2.6 %multiply_bitcast_fusion.2 = (f32[332,268]{0,1:T(8,128)}, f32[1,332,268]{1,2,0:T(8,128)S(1)}, f32[1,332,268]{1,2,0:T(8,128)S(1)}) fusion(f32[1,332,268]{1,2,0:T(8,128)} %divide_add_fusion, f32[1,332,268]{1,2,0:T(8,128)} %get-tuple-element.66, f32[8,332,268]{1,2,0:T(8,128)S(1)} %pad_maximum_fusion, pred[268]{0:T(512)(128)(4,1)S(1)} %fusion.39, ...), kind=kLoop, calls=%fused_computation.67 | loop fusion | flops 1067712 | bytes 3915544 | tf_op jit(solution)/shard_map/reduce_sum | solution.py:168
  113.5 9.2 %scatter_fusion.1 = f32[332,268]{0,1:T(8,128)} fusion(f32[332,268]{0,1:T(8,128)} %fusion.23, s32[64]{0:T(128)S(1)} %get-tuple-element.110, f32[64]{0:T(128)S(1)} %get-tuple-element.107), kind=kCustom, calls=%fused_computation.4 | custom fusion | flops 64 | bytes 1280 | tf_op jit(solution)/shard_map/scatter-add | solution.py:146
  122.7 2.4 %multiply_bitcast_fusion.1 = (f32[332,268]{0,1:T(8,128)}, f32[1,332,268]{1,2,0:T(8,128)S(1)}, f32[1,332,268]{1,2,0:T(8,128)S(1)}) fusion(f32[1,332,268]{1,2,0:T(8,128)} %get-tuple-element.65, f32[8,332,268]{1,2,0:T(8,128)S(1)} %pad_maximum_fusion, pred[268]{0:T(512)(128)(4,1)S(1)} %fusion.39, pred[332]{0:T(512)(128)(4,1)S(1)} %fusion.38, ...), kind=kLoop, calls=%fused_computation.66 | loop fusion | flops 800784 | bytes 3559640 | tf_op jit(solution)/shard_map/reduce_sum | solution.py:168
  126.3 9.1 %scatter_fusion.2 = f32[332,268]{0,1:T(8,128)} fusion(f32[332,268]{0,1:T(8,128)} %fusion.21, s32[64]{0:T(128)S(1)} %get-tuple-element.110, f32[64]{0:T(128)S(1)} %get-tuple-element.62), kind=kCustom, calls=%fused_computation.5 | custom fusion | flops 64 | bytes 1280 | tf_op jit(solution)/shard_map/scatter-add | solution.py:146
  135.4 2.6 %multiply_bitcast_fusion = (f32[332,268]{0,1:T(8,128)S(1)}, f32[1,332,268]{1,2,0:T(8,128)}, f32[1,332,268]{1,2,0:T(8,128)}, f32[1,332,268]{1,2,0:T(8,128)S(1)}) fusion(f32[8,332,268]{1,2,0:T(8,128)S(1)} %pad_maximum_fusion, pred[268]{0:T(512)(128)(4,1)S(1)} %fusion.39, pred[332]{0:T(512)(128)(4,1)S(1)} %fusion.38, f32[1,332,268]{1,2,0:T(8,128)} %copy-done.26, ...), kind=kLoop, calls=%fused_computation.64 | loop fusion | flops 978736 | bytes 4627352 | tf_op jit(solution)/shard_map/reduce_sum | solution.py:168
  138.1 3.3 %fusion.32 = (f32[1,332,268]{1,2,0:T(8,128)S(1)}, f32[1,332,268]{1,2,0:T(8,128)S(1)}, f32[332,268]{0,1:T(8,128)S(1)}, f32[332,268]{0,1:T(8,128)S(1)}, f32[332,268]{0,1:T(8,128)S(1)}, /*index=5*/f32[1,332,268]{1,2,0:T(8,128)S(1)}) fusion(f32[1,332,268]{1,2,0:T(8,128)S(1)} %get-tuple-element.61, f32[1,332,268]{1,2,0:T(8,128)S(1)} %copy-done.32, ...), kind=kLoop, calls=%fused_computation.139 | loop fusion | flops 12723568 | bytes 4626752 | tf_op jit(solution)/shard_map/sub | solution.py:40
  143.2 17.1 %all-reduce.9.cloned.1.call-done = f32[2,320,256]{1,2,0:T(8,128)} async-done(((f32[2,320,256]{1,2,0:T(8,128)}), f32[2,320,256]{1,2,0:T(8,128)}) %all-reduce.9.cloned.1.call-update) | async-done | bytes 655376 | tf_op jit(solution)/shard_map/psum | solution.py:217
  161.5 3.7 %collective-permute-start.4 = (f32[2,1,256]{1,2,0:T(8,128)S(1)}, f32[2,1,256]{1,2,0:T(8,128)S(1)}, u32[]{:S(2)}, u32[]{:S(2)}) collective-permute-start(f32[2,1,256]{1,2,0:T(8,128)S(1)} %get-tuple-element.97), channel_id=1, source_target_pairs={{0,2},{2,4},{4,6},{1,3},{3,5},{5,7},{8,10},{10,12},{12,14},{9,11},... | collective-permute-start | bytes 6152 | tf_op jit(solution)/shard_map/ppermute | solution.py:18
  165.3 1.6 collective-permute-start.5
  166.8 4.3 %collective-permute-done.4 = f32[2,1,256]{1,2,0:T(8,128)S(1)} collective-permute-done((f32[2,1,256]{1,2,0:T(8,128)S(1)}, f32[2,1,256]{1,2,0:T(8,128)S(1)}, u32[]{:S(2)}, u32[]{:S(2)}) %collective-permute-start.4) | collective-permute-done | bytes 2080 | tf_op jit(solution)/shard_map/ppermute | solution.py:18
  171.2 4.5 %collective-permute-done.5 = f32[2,1,256]{1,2,0:T(8,128)S(1)} collective-permute-done((f32[2,1,256]{1,2,0:T(8,128)S(1)}, f32[2,1,256]{1,2,0:T(8,128)S(1)}, u32[]{:S(2)}, u32[]{:S(2)}) %collective-permute-start.5) | collective-permute-done | bytes 2080 | tf_op jit(solution)/shard_map/ppermute | solution.py:20
  176.5 3.4 %collective-permute-start.6 = (f32[2,322,1]{1,2,0:T(1,128)S(1)}, f32[2,322,1]{1,2,0:T(1,128)S(1)}, u32[]{:S(2)}, u32[]{:S(2)}) collective-permute-start(f32[2,322,1]{1,2,0:T(1,128)S(1)} %get-tuple-element.91), channel_id=1, source_target_pairs={{0,1},{2,3},{4,5},{6,7},{8,9},{10,11},{12,13},{14,15},{16,17},{18,... | collective-permute-start | bytes 7736 | tf_op jit(solution)/shard_map/ppermute | solution.py:18
  181.2 4.2 %collective-permute-done.7 = f32[2,322,1]{1,2,0:T(1,128)S(1)} collective-permute-done((f32[2,322,1]{1,2,0:T(1,128)S(1)}, f32[2,322,1]{1,2,0:T(1,128)S(1)}, u32[]{:S(2)}, u32[]{:S(2)}) %collective-permute-start.7) | collective-permute-done | bytes 2608 | tf_op jit(solution)/shard_map/ppermute | solution.py:20
  185.3 3.5 %fusion.9 = f32[2,320,256]{1,2,0:T(8,128)S(1)} fusion(f32[2,320,256]{1,2,0:T(8,128)} %all-reduce.9.cloned.1.call-done, f32[2,322,1]{1,2,0:T(1,128)S(1)} %collective-permute-done.7, f32[2,1,256]{1,2,0:T(8,128)S(1)} %collective-permute-done.5, f32[2,1,256]{1,2,0:T(8,128)S(1)} %collective-permute-done.4, f32[2,322,1]{1,2,0:T(1,128)S(1)} %collective-permute-done.6), kind=kLoop, calls=%fused_computation.29 | loop fusion | flops 2457600 | bytes 1319968 | tf_op jit(solution)/shard_map/add | solution.py:61
  189.0 3.4 %collective-permute-start.8 = (f32[2,1,256]{1,2,0:T(8,128)S(1)}, f32[2,1,256]{1,2,0:T(8,128)S(1)}, u32[]{:S(2)}, u32[]{:S(2)}) collective-permute-start(f32[2,1,256]{1,2,0:T(8,128)S(1)} %get-tuple-element.95), channel_id=1, source_target_pairs={{0,2},{2,4},{4,6},{1,3},{3,5},{5,7},{8,10},{10,12},{12,14},{9,11},... | collective-permute-start | bytes 6152 | tf_op jit(solution)/shard_map/ppermute | solution.py:18
  193.7 2.5 %collective-permute-done.8 = f32[2,1,256]{1,2,0:T(8,128)S(1)} collective-permute-done((f32[2,1,256]{1,2,0:T(8,128)S(1)}, f32[2,1,256]{1,2,0:T(8,128)S(1)}, u32[]{:S(2)}, u32[]{:S(2)}) %collective-permute-start.8) | collective-permute-done | bytes 2080 | tf_op jit(solution)/shard_map/ppermute | solution.py:18
  196.2 4.4 %collective-permute-done.9 = f32[2,1,256]{1,2,0:T(8,128)S(1)} collective-permute-done((f32[2,1,256]{1,2,0:T(8,128)S(1)}, f32[2,1,256]{1,2,0:T(8,128)S(1)}, u32[]{:S(2)}, u32[]{:S(2)}) %collective-permute-start.9) | collective-permute-done | bytes 2080 | tf_op jit(solution)/shard_map/ppermute | solution.py:20
  200.7 1.7 collective-permute-start.10
  203.8 1.5 slice_subtract_fusion.12
  207.9 1.9 fusion.3
  (151 shorter events, 32.6 us)
Async XLA Ops:
  7.2 11.5 %copy-start.44 = (f32[1,320,256]{2,1,0:T(8,128)S(1)}, f32[1,320,256]{2,1,0:T(8,128)}, u32[]{:S(2)}) copy-start(f32[1,320,256]{2,1,0:T(8,128)} %param.32) | copy-start | bytes 983044
  7.2 12.4 %copy-start.45 = (f32[1,320,256]{2,1,0:T(8,128)S(1)}, f32[1,320,256]{2,1,0:T(8,128)}, u32[]{:S(2)}) copy-start(f32[1,320,256]{2,1,0:T(8,128)} %param.33) | copy-start | bytes 983044
  7.2 153.2 %all-reduce.9.cloned.1.call-start = ((), (), s32[]{:S(2)}) async-start(), calls=%async_computation | async-start | bytes 1572864 | tf_op jit(solution)/shard_map/psum | solution.py:217
  19.8 14.1 %copy-start.42 = (f32[1,320,256]{1,2,0:T(8,128)S(1)}, f32[1,320,256]{1,2,0:T(8,128)}, u32[]{:S(2)}) copy-start(f32[1,320,256]{1,2,0:T(8,128)} %copy.82) | copy-start | bytes 983044
  19.8 14.1 %copy-start.41 = (f32[1,320,256]{1,2,0:T(8,128)S(1)}, f32[1,320,256]{1,2,0:T(8,128)}, u32[]{:S(2)}) copy-start(f32[1,320,256]{1,2,0:T(8,128)} %copy.83) | copy-start | bytes 983044
  19.8 14.2 %copy-start.40 = (f32[1,320,256]{1,2,0:T(8,128)S(1)}, f32[1,320,256]{1,2,0:T(8,128)}, u32[]{:S(2)}) copy-start(f32[1,320,256]{1,2,0:T(8,128)} %copy.84) | copy-start | bytes 983044
  34.1 21.4 %copy-start = (f32[8,320,256]{1,2,0:T(8,128)}, f32[8,320,256]{1,2,0:T(8,128)S(1)}, u32[]{:S(2)}) copy-start(f32[8,320,256]{1,2,0:T(8,128)S(1)} %constant_dynamic-update-slice_fusion) | copy-start | bytes 7864324
  34.1 13.2 %copy-start.46 = (f32[1,3,1]{1,2,0:T(1,128)S(1)}, f32[1,3,1]{1,2,0:T(1,128)}, u32[]{:S(2)}) copy-start(f32[1,3,1]{1,2,0:T(1,128)} %param.26) | copy-start | bytes 40
  34.1 13.9 %copy-start.47 = (s32[64]{0:T(128)S(1)}, s32[64]{0:T(128)}, u32[]{:S(2)}) copy-start(s32[64]{0:T(128)} %param.27) | copy-start | bytes 772
  34.1 13.9 %copy-start.48 = (s32[64]{0:T(128)S(1)}, s32[64]{0:T(128)}, u32[]{:S(2)}) copy-start(s32[64]{0:T(128)} %param.28) | copy-start | bytes 772
  34.1 13.9 %copy-start.50 = (s32[3]{0:T(128)S(1)}, s32[3]{0:T(128)}, u32[]{:S(2)}) copy-start(s32[3]{0:T(128)} %constant.129.clone.1) | copy-start | bytes 40
  37.6 16.6 %collective-permute-start.1 = (f32[8,6,256]{2,0,1:T(8,128)S(1)}, f32[8,6,256]{2,0,1:T(8,128)S(1)}, u32[]{:S(2)}, u32[]{:S(2)}) collective-permute-start(f32[8,6,256]{2,0,1:T(8,128)S(1)} %copy.87), channel_id=1, source_target_pairs={{2,0},{4,2},{6,4},{3,1},{5,3},{7,5},{10,8},{12,10},{14,12},{11,9},... | collective-permute-start | bytes 147464 | tf_op jit(solution)/shard_map/ppermute | solution.py:20
  40.4 12.4 %collective-permute-start = (f32[8,6,256]{2,0,1:T(8,128)S(1)}, f32[8,6,256]{2,0,1:T(8,128)S(1)}, u32[]{:S(2)}, u32[]{:S(2)}) collective-permute-start(f32[8,6,256]{2,0,1:T(8,128)S(1)} %copy.86), channel_id=1, source_target_pairs={{0,2},{2,4},{4,6},{1,3},{3,5},{5,7},{8,10},{10,12},{12,14},{9,11},... | collective-permute-start | bytes 147464 | tf_op jit(solution)/shard_map/ppermute | solution.py:18
  55.5 11.5 %copy-start.16 = (f32[8,6,256]{1,2,0:T(8,128)S(1)}, f32[8,6,256]{1,2,0:T(8,128)}, u32[]{:S(2)}) copy-start(f32[8,6,256]{1,2,0:T(8,128)} %copy.88) | copy-start | bytes 147460
  55.5 11.5 %copy-start.17 = (f32[8,6,256]{1,2,0:T(8,128)S(1)}, f32[8,6,256]{1,2,0:T(8,128)}, u32[]{:S(2)}) copy-start(f32[8,6,256]{1,2,0:T(8,128)} %copy.89) | copy-start | bytes 147460
  56.6 6.0 %collective-permute-start.2 = (f32[8,332,6]{1,2,0:T(8,128)S(1)}, f32[8,332,6]{1,2,0:T(8,128)S(1)}, u32[]{:S(2)}, u32[]{:S(2)}) collective-permute-start(f32[8,332,6]{1,2,0:T(8,128)S(1)} %get-tuple-element.81), channel_id=1, source_target_pairs={{0,1},{2,3},{4,5},{6,7},{8,9},{10,11},{12,13},{14,15},{16,17},{18,... | collective-permute-start | bytes 191240 | tf_op jit(solution)/shard_map/ppermute | solution.py:18
  60.4 6.5 %collective-permute-start.3 = (f32[8,332,6]{1,2,0:T(8,128)S(1)}, f32[8,332,6]{1,2,0:T(8,128)S(1)}, u32[]{:S(2)}, u32[]{:S(2)}) collective-permute-start(f32[8,332,6]{1,2,0:T(8,128)S(1)} %get-tuple-element.82), channel_id=1, source_target_pairs={{1,0},{3,2},{5,4},{7,6},{9,8},{11,10},{13,12},{15,14},{17,16},{19,... | collective-permute-start | bytes 191240 | tf_op jit(solution)/shard_map/ppermute | solution.py:20
  70.2 2.7 %copy-start.31 = (f32[1,332,268]{1,2,0:T(8,128)}, f32[1,332,268]{1,2,0:T(8,128)S(1)}, u32[]{:S(2)}) copy-start(f32[1,332,268]{1,2,0:T(8,128)S(1)} %get-tuple-element.86) | copy-start | bytes 1067716
  90.3 10.2 %copy-start.49 = (f32[1,3,64]{2,0,1:T(1,128)S(1)}, f32[1,3,64]{2,0,1:T(1,128)}, u32[]{:S(2)}) copy-start(f32[1,3,64]{2,0,1:T(1,128)} %param.29) | copy-start | bytes 2308
  109.6 2.6 %copy-start.8 = (f32[1,332,268]{1,2,0:T(8,128)S(1)}, f32[1,332,268]{1,2,0:T(8,128)}, u32[]{:S(2)}) copy-start(f32[1,332,268]{1,2,0:T(8,128)} %get-tuple-element.70) | copy-start | bytes 1067716
  109.6 2.6 %copy-start.11 = (f32[1,332,268]{1,2,0:T(8,128)S(1)}, f32[1,332,268]{1,2,0:T(8,128)}, u32[]{:S(2)}) copy-start(f32[1,332,268]{1,2,0:T(8,128)} %get-tuple-element.71) | copy-start | bytes 1067716
  109.6 2.6 %copy-start.18 = (f32[332,268]{0,1:T(8,128)S(1)}, f32[332,268]{0,1:T(8,128)}, u32[]{:S(2)}) copy-start(f32[332,268]{0,1:T(8,128)} %scatter_fusion) | copy-start | bytes 1067716
  135.4 2.6 %copy-start.1 = (f32[1,332,268]{1,2,0:T(8,128)S(1)}, f32[1,332,268]{1,2,0:T(8,128)}, u32[]{:S(2)}) copy-start(f32[1,332,268]{1,2,0:T(8,128)} %divide_add_fusion) | copy-start | bytes 1067716
  135.4 2.6 %copy-start.15 = (f32[1,332,268]{1,2,0:T(8,128)S(1)}, f32[1,332,268]{1,2,0:T(8,128)}, u32[]{:S(2)}) copy-start(f32[1,332,268]{1,2,0:T(8,128)} %copy-done.14) | copy-start | bytes 1067716
  135.4 2.6 %copy-start.23 = (f32[332,268]{0,1:T(8,128)S(1)}, f32[332,268]{0,1:T(8,128)}, u32[]{:S(2)}) copy-start(f32[332,268]{0,1:T(8,128)} %copy-done.22) | copy-start | bytes 1067716
  135.4 2.7 %copy-start.28 = (f32[1,332,268]{1,2,0:T(8,128)S(1)}, f32[1,332,268]{1,2,0:T(8,128)}, u32[]{:S(2)}) copy-start(f32[1,332,268]{1,2,0:T(8,128)} %copy-done.27) | copy-start | bytes 1067716
  135.4 2.7 %copy-start.30 = (f32[1,332,268]{1,2,0:T(8,128)S(1)}, f32[1,332,268]{1,2,0:T(8,128)}, u32[]{:S(2)}) copy-start(f32[1,332,268]{1,2,0:T(8,128)} %copy-done.29) | copy-start | bytes 1067716
  135.4 2.7 %copy-start.32 = (f32[1,332,268]{1,2,0:T(8,128)S(1)}, f32[1,332,268]{1,2,0:T(8,128)}, u32[]{:S(2)}) copy-start(f32[1,332,268]{1,2,0:T(8,128)} %copy-done.31) | copy-start | bytes 1067716
  138.0 4.3 %copy-start.24 = (f32[1,332,268]{1,2,0:T(8,128)}, f32[1,332,268]{1,2,0:T(8,128)S(1)}, u32[]{:S(2)}) copy-start(f32[1,332,268]{1,2,0:T(8,128)S(1)} %get-tuple-element.61) | copy-start | bytes 1067716
  138.0 3.4 %copy-start.36 = (f32[332,268]{0,1:T(8,128)S(1)}, f32[332,268]{0,1:T(8,128)}, u32[]{:S(2)}) copy-start(f32[332,268]{0,1:T(8,128)} %get-tuple-element.52) | copy-start | bytes 1067716
  138.0 3.4 %copy-start.37 = (f32[332,268]{0,1:T(8,128)S(1)}, f32[332,268]{0,1:T(8,128)}, u32[]{:S(2)}) copy-start(f32[332,268]{0,1:T(8,128)} %get-tuple-element.55) | copy-start | bytes 1067716
  143.2 50.5 %copy-start.25 = (f32[1,332,268]{1,2,0:T(8,128)S(1)}, f32[1,332,268]{1,2,0:T(8,128)}, u32[]{:S(2)}) copy-start(f32[1,332,268]{1,2,0:T(8,128)} %copy-done.24) | copy-start | bytes 1067716
  161.5 9.7 %collective-permute-start.4 = (f32[2,1,256]{1,2,0:T(8,128)S(1)}, f32[2,1,256]{1,2,0:T(8,128)S(1)}, u32[]{:S(2)}, u32[]{:S(2)}) collective-permute-start(f32[2,1,256]{1,2,0:T(8,128)S(1)} %get-tuple-element.97), channel_id=1, source_target_pairs={{0,2},{2,4},{4,6},{1,3},{3,5},{5,7},{8,10},{10,12},{12,14},{9,11},... | collective-permute-start | bytes 6152 | tf_op jit(solution)/shard_map/ppermute | solution.py:18
  165.2 38.5 %copy-start.4 = (f32[1,332,268]{1,2,0:T(8,128)S(1)}, f32[1,332,268]{1,2,0:T(8,128)}, u32[]{:S(2)}) copy-start(f32[1,332,268]{1,2,0:T(8,128)} %get-tuple-element.68) | copy-start | bytes 1067716
  165.2 38.5 %copy-start.7 = (f32[1,332,268]{1,2,0:T(8,128)S(1)}, f32[1,332,268]{1,2,0:T(8,128)}, u32[]{:S(2)}) copy-start(f32[1,332,268]{1,2,0:T(8,128)} %get-tuple-element.69) | copy-start | bytes 1067716
  165.2 38.5 %copy-start.10 = (f32[1,332,268]{1,2,0:T(8,128)S(1)}, f32[1,332,268]{1,2,0:T(8,128)}, u32[]{:S(2)}) copy-start(f32[1,332,268]{1,2,0:T(8,128)} %get-tuple-element.70) | copy-start | bytes 1067716
  165.2 38.5 %copy-start.13 = (f32[1,332,268]{1,2,0:T(8,128)S(1)}, f32[1,332,268]{1,2,0:T(8,128)}, u32[]{:S(2)}) copy-start(f32[1,332,268]{1,2,0:T(8,128)} %get-tuple-element.71) | copy-start | bytes 1067716
  165.3 38.5 %copy-start.20 = (f32[332,268]{0,1:T(8,128)S(1)}, f32[332,268]{0,1:T(8,128)}, u32[]{:S(2)}) copy-start(f32[332,268]{0,1:T(8,128)} %scatter_fusion.2) | copy-start | bytes 1067716
  165.3 38.5 %copy-start.38 = (f32[1,332,268]{1,2,0:T(8,128)S(1)}, f32[1,332,268]{1,2,0:T(8,128)}, u32[]{:S(2)}) copy-start(f32[1,332,268]{1,2,0:T(8,128)} %get-tuple-element.59) | copy-start | bytes 1067716
  165.3 38.5 %copy-start.39 = (f32[1,332,268]{1,2,0:T(8,128)S(1)}, f32[1,332,268]{1,2,0:T(8,128)}, u32[]{:S(2)}) copy-start(f32[1,332,268]{1,2,0:T(8,128)} %get-tuple-element.60) | copy-start | bytes 1067716
  165.3 10.3 %collective-permute-start.5 = (f32[2,1,256]{1,2,0:T(8,128)S(1)}, f32[2,1,256]{1,2,0:T(8,128)S(1)}, u32[]{:S(2)}, u32[]{:S(2)}) collective-permute-start(f32[2,1,256]{1,2,0:T(8,128)S(1)} %get-tuple-element.98), channel_id=1, source_target_pairs={{2,0},{4,2},{6,4},{3,1},{5,3},{7,5},{10,8},{12,10},{14,12},{11,9},... | collective-permute-start | bytes 6152 | tf_op jit(solution)/shard_map/ppermute | solution.py:20
  176.5 4.7 %collective-permute-start.6 = (f32[2,322,1]{1,2,0:T(1,128)S(1)}, f32[2,322,1]{1,2,0:T(1,128)S(1)}, u32[]{:S(2)}, u32[]{:S(2)}) collective-permute-start(f32[2,322,1]{1,2,0:T(1,128)S(1)} %get-tuple-element.91), channel_id=1, source_target_pairs={{0,1},{2,3},{4,5},{6,7},{8,9},{10,11},{12,13},{14,15},{16,17},{18,... | collective-permute-start | bytes 7736 | tf_op jit(solution)/shard_map/ppermute | solution.py:18
  179.9 5.5 %collective-permute-start.7 = (f32[2,322,1]{1,2,0:T(1,128)S(1)}, f32[2,322,1]{1,2,0:T(1,128)S(1)}, u32[]{:S(2)}, u32[]{:S(2)}) collective-permute-start(f32[2,322,1]{1,2,0:T(1,128)S(1)} %get-tuple-element.92), channel_id=1, source_target_pairs={{1,0},{3,2},{5,4},{7,6},{9,8},{11,10},{13,12},{15,14},{17,16},{19,... | collective-permute-start | bytes 7736 | tf_op jit(solution)/shard_map/ppermute | solution.py:20
  189.0 7.3 %collective-permute-start.8 = (f32[2,1,256]{1,2,0:T(8,128)S(1)}, f32[2,1,256]{1,2,0:T(8,128)S(1)}, u32[]{:S(2)}, u32[]{:S(2)}) collective-permute-start(f32[2,1,256]{1,2,0:T(8,128)S(1)} %get-tuple-element.95), channel_id=1, source_target_pairs={{0,2},{2,4},{4,6},{1,3},{3,5},{5,7},{8,10},{10,12},{12,14},{9,11},... | collective-permute-start | bytes 6152 | tf_op jit(solution)/shard_map/ppermute | solution.py:18
  192.4 8.3 %collective-permute-start.9 = (f32[2,1,256]{1,2,0:T(8,128)S(1)}, f32[2,1,256]{1,2,0:T(8,128)S(1)}, u32[]{:S(2)}, u32[]{:S(2)}) collective-permute-start(f32[2,1,256]{1,2,0:T(8,128)S(1)} %get-tuple-element.96), channel_id=1, source_target_pairs={{2,0},{4,2},{6,4},{3,1},{5,3},{7,5},{10,8},{12,10},{14,12},{11,9},... | collective-permute-start | bytes 6152 | tf_op jit(solution)/shard_map/ppermute | solution.py:20
  200.6 3.1 %copy-start.43 = (f32[2,1,256]{1,2,0:T(8,128)}, f32[2,1,256]{1,2,0:T(8,128)S(1)}, u32[]{:S(2)}) copy-start(f32[2,1,256]{1,2,0:T(8,128)S(1)} %collective-permute-done.9) | copy-start | bytes 6148
  200.7 6.3 %collective-permute-start.10 = (f32[2,322,1]{1,2,0:T(1,128)S(1)}, f32[2,322,1]{1,2,0:T(1,128)S(1)}, u32[]{:S(2)}, u32[]{:S(2)}) collective-permute-start(f32[2,322,1]{1,2,0:T(1,128)S(1)} %get-tuple-element.89), channel_id=1, source_target_pairs={{0,1},{2,3},{4,5},{6,7},{8,9},{10,11},{12,13},{14,15},{16,17},{18,... | collective-permute-start | bytes 7736 | tf_op jit(solution)/shard_map/ppermute | solution.py:18
  202.4 5.5 %collective-permute-start.11 = (f32[2,322,1]{1,2,0:T(1,128)S(1)}, f32[2,322,1]{1,2,0:T(1,128)S(1)}, u32[]{:S(2)}, u32[]{:S(2)}) collective-permute-start(f32[2,322,1]{1,2,0:T(1,128)S(1)} %get-tuple-element.90), channel_id=1, source_target_pairs={{1,0},{3,2},{5,4},{7,6},{9,8},{11,10},{13,12},{15,14},{17,16},{19,... | collective-permute-start | bytes 7736 | tf_op jit(solution)/shard_map/ppermute | solution.py:20
  (16 other events, 26.1 us)
Sparse Core Ops, SparseCore 0:
  143.4 16.9 all-reduce.8
where the time goes:
time: 220 us; the launch traced here: 218 us
  other arithmetic  81.3 us (37%)
  local copies, waits for them, and re-layouts  43.8 us (20%)
  waiting for transfers between devices  43 us (20%)
  starting transfers between devices  29.6 us (13%)
  between operations  20.8 us (9%)
    scatter-add x3, other arithmetic, inject(): return adjoint_field.at[:, obs_lx, obs_ly].add(mismatch)  27.4 us
    ppermute x6, starting transfers between devices, padded_2(): lax.ppermute(tail, axis, [(i, (i + 1) % count) for i in range(ends)])  21.5 us
    unnamed x118, local copies, waits for them, and re-layouts  20.3 us
    ppermute x6, waiting for transfers between devices, padded_2(): lax.ppermute(head, axis, [((i + 1) % count, i) for i in range(ends)])  18.2 us
    psum x1, waiting for transfers between devices, on_device(): summed = lax.psum(stacked, 'test')  17.1 us
    unnamed x2, other arithmetic  11.8 us
    ppermute x6, starting transfers between devices, padded_2(): lax.ppermute(head, axis, [((i + 1) % count, i) for i in range(ends)])  8.02 us
    ppermute x6, waiting for transfers between devices, padded_2(): lax.ppermute(tail, axis, [(i, (i + 1) % count) for i in range(ends)])  7.71 us
  transfers between devices with their start and end apart: 13, of which 9 were waited for; matrix products, arithmetic and copies ran while one was open for 4% of the time, Pallas kernels for 0%

commit v1 on v0

--- a/solution.py
+++ b/solution.py
@@ -214,7 +214,8 @@
         matrix_end,
     )
     stacked = jnp.stack([grad_cond, grad_shape], 0)
-    summed = lax.psum(stacked, "test")
+    parts = lax.all_gather(stacked, "test")
+    summed = jnp.sum(parts, axis=0)
     smoothed = smooth(summed)
     return (smoothed[0], smoothed[1], fracture_adj, matrix_adj)
 

time: 220 us -> 209 us (0.950)
  waiting for transfers between devices: 43 us -> 32.5 us
  other arithmetic: 81.3 us -> 78.2 us
  local copies, waits for them, and re-layouts: 43.8 us -> 46.2 us
    psum x1 -> x0, waiting for transfers between devices: 17.1 us -> none  [on_device(): summed = lax.psum(stacked, 'test')]
    all_gather x0 -> x1, waiting for transfers between devices: none -> 7.38 us  [on_device(): parts = lax.all_gather(stacked, 'test')]
    add x2, other arithmetic: 5.42 us -> 1.67 us  [smooth(): grad_field + blend_rate * (nearby[0] + nearby[1] + nearby[2] + nearby[3]...]
    unnamed x118 -> x117, local copies, waits for them, and re-layouts: 20.3 us -> 22.6 us
  transfers between devices with their start and end apart: 13 -> 13, of which waited for: 9 -> 8; matrix products, arithmetic and copies ran while one was open for 4% -> 5% of each run, Pallas kernels for 0% -> 0%
where the time goes in v1:
time: 209 us; the launch traced here: 207 us
  other arithmetic  78.2 us (37%)
  local copies, waits for them, and re-layouts  46.2 us (22%)
  waiting for transfers between devices  32.5 us (16%)
  starting transfers between devices  29.8 us (14%)
  between operations  20.4 us (10%)
    scatter-add x3, other arithmetic, inject(): return adjoint_field.at[:, obs_lx, obs_ly].add(mismatch)  27.3 us
    unnamed x117, local copies, waits for them, and re-layouts  22.6 us
    ppermute x6, starting transfers between devices, padded_2(): lax.ppermute(tail, axis, [(i, (i + 1) % count) for i in range(ends)])  21.5 us
    ppermute x6, waiting for transfers between devices, padded_2(): lax.ppermute(head, axis, [((i + 1) % count, i) for i in range(ends)])  17.4 us
    unnamed x2, other arithmetic  11.9 us
    ppermute x6, starting transfers between devices, padded_2(): lax.ppermute(head, axis, [((i + 1) % count, i) for i in range(ends)])  8.24 us
    ppermute x6, waiting for transfers between devices, padded_2(): lax.ppermute(tail, axis, [(i, (i + 1) % count) for i in range(ends)])  7.74 us
    reduce_sum x3, other arithmetic, margin_window(): jnp.sum(swap_rate * (fracture - matrix), axis=0)  7.54 us
  transfers between devices with their start and end apart: 13, of which 8 were waited for; matrix products, arithmetic and copies ran while one was open for 5% of the time, Pallas kernels for 0%

profile of v1, /device:TPU:0, one launch (start us, length us, event | category | flops | bytes accessed | tf_op | source)
XLA Modules:
  0.0 207.1 jit_solution(12476625196430995167)
XLA Ops:
  7.2 2.0 fusion.52
  9.2 1.9 copy.68
  11.1 1.9 copy.69
  13.0 1.9 copy.70
  14.9 1.9 copy.78
  16.8 1.9 copy.79
  22.0 6.5 %bitcast_dynamic-update-slice_fusion.1 = (f32[8,320,256]{1,2,0:T(8,128)S(1)}, pred[320,256]{0,1:T(8,128)(4,1)S(1)}, pred[320,256]{0,1:T(8,128)(4,1)S(1)}, pred[3...) fusion(f32[8,320,256]{1,2,0:T(8,128)S(1)} %bitcast_dynamic-upda, ...), kind=kLoop, calls=%fused_computation.121 | loop fusion | flops 1310720 | bytes 1507360
  28.5 5.4 %bitcast_dynamic-update-slice_fusion = f32[8,320,256]{1,2,0:T(8,128)S(1)} fusion(f32[8,320,256]{1,2,0:T(8,128)S(1)} %get-tuple-element.72, pred[320,256]{0,1:T(8,128)(4,1)S(1)} %get-tuple-element.80, pred[320,256]{0,1:T(8,128)(4,1)S(1)} %get-tuple-element.79, pred[320,256]{0,1:T(8,128)(4,1)S(1)} %get-tuple-element.78, ...), kind=kLoop, calls=%fused_computation.120 | loop fusion | flops 655360 | bytes 1179680
  34.2 1.9 fusion.49
  36.1 1.5 copy.83
  38.9 1.6 copy.82
  40.5 5.6 %collective-permute-start = (f32[8,6,256]{2,0,1:T(8,128)S(1)}, f32[8,6,256]{2,0,1:T(8,128)S(1)}, u32[]{:S(2)}, u32[]{:S(2)}) collective-permute-start(f32[8,6,256]{2,0,1:T(8,128)S(1)} %copy.82), channel_id=1, source_target_pairs={{0,2},{2,4},{4,6},{1,3},{3,5},{5,7},{8,10},{10,12},{12,14},{9,11},... | collective-permute-start | bytes 147464 | tf_op jit(solution)/shard_map/ppermute | solution.py:18
  56.2 3.8 %collective-permute-start.2 = (f32[8,332,6]{1,2,0:T(8,128)S(1)}, f32[8,332,6]{1,2,0:T(8,128)S(1)}, u32[]{:S(2)}, u32[]{:S(2)}) collective-permute-start(f32[8,332,6]{1,2,0:T(8,128)S(1)} %get-tuple-element.81), channel_id=1, source_target_pairs={{0,1},{2,3},{4,5},{6,7},{8,9},{10,11},{12,13},{14,15},{16,17},{18,... | collective-permute-start | bytes 191240 | tf_op jit(solution)/shard_map/ppermute | solution.py:18
  62.3 4.3 %collective-permute-done.3 = f32[8,332,6]{1,2,0:T(8,128)S(1)} collective-permute-done((f32[8,332,6]{1,2,0:T(8,128)S(1)}, f32[8,332,6]{1,2,0:T(8,128)S(1)}, u32[]{:S(2)}, u32[]{:S(2)}) %collective-permute-start.3) | collective-permute-done | bytes 63776 | tf_op jit(solution)/shard_map/ppermute | solution.py:20
  66.6 3.2 %pad_maximum_fusion = f32[8,332,268]{1,2,0:T(8,128)S(1)} fusion(f32[8,332,6]{1,2,0:T(8,128)S(1)} %collective-permute-done.3, f32[8,6,256]{1,2,0:T(8,128)S(1)} %copy-done.17, f32[8,320,256]{1,2,0:T(8,128)} %copy-done, f32[8,6,256]{1,2,0:T(8,128)S(1)} %copy-done.16, f32[8,332,6]{1,2,0:T(8,128)S(1)} %collective-permute-done.2), kind=kLoop, calls=%fused_computation.6 | loop fusion | flops 2847232 | bytes 5694464 | tf_op jit(solution)/shard_map/concatenate | solution.py:16
  70.6 1.9 add_subtract_fusion.2
  77.9 2.8 %add_subtract_fusion.1 = (f32[1,332,268]{1,2,0:T(8,128)S(1)}, f32[1,332,268]{1,2,0:T(8,128)}, f32[1,332,268]{1,2,0:T(8,128)}) fusion(f32[1,332,268]{1,2,0:T(8,128)} %get-tuple-element.71, f32[1,332,268]{1,2,0:T(8,128)} %get-tuple-element.70, f32[1,332,268]{1,2,0:T(8,128)} %get-tuple-element.69, f32[1,332,268]{1,2,0:T(8,128)} %get-tuple-element.68, ...), kind=kLoop, calls=%fused_computation.82 | loop fusion | flops 1779520 | bytes 4271448 | tf_op jit(solution)/shard_map/sub | solution.py:137
  82.0 2.0 add.292
  84.0 2.0 divide_add_fusion
  86.0 1.9 gather_fusion.2
  87.9 1.9 gather_fusion.1
  89.8 2.8 %multiply_subtract_fusion = f32[1,332,268]{1,2,0:T(8,128)S(1)} fusion(f32[1,332,268]{1,2,0:T(8,128)} %get-tuple-element.71, f32[1,332,268]{1,2,0:T(8,128)} %get-tuple-element.70, f32[1,332,268]{1,2,0:T(8,128)} %get-tuple-element.69, f32[1,332,268]{1,2,0:T(8,128)} %get-tuple-element.68, f32[8,332,268]{1,2,0:T(8,128)S(1)} %pad_maximum_fusion, ...), kind=kLoop, calls=%fused_computation.74 | loop fusion | flops 1690544 | bytes 3559640 | tf_op jit(solution)/shard_map/sub | solution.py:137
  94.0 2.1 %add.303 = f32[1,332,268]{1,2,0:T(8,128)} dynamic-update-slice(f32[1,332,268]{1,2,0:T(8,128)} %copy-done.33, f32[1,1,1]{1,2,0:T(1,128)} %fusion.55, s32[]{:T(128)} %constant.116.clone.1, s32[]{:T(128)} %bitcast.27, s32[]{:T(128)} %bitcast.29) | dynamic-update-slice | bytes 12 | tf_op jit(solution)/shard_map/add | solution.py:137
  96.1 2.2 %add_bitcast_fusion.3 = (f32[332,268]{0,1:T(8,128)}, f32[332,268]{0,1:T(8,128)}) fusion(f32[1,332,268]{1,2,0:T(8,128)} %divide_add_fusion, f32[1,332,268]{1,2,0:T(8,128)} %add.303, f32[8,332,268]{1,2,0:T(8,128)S(1)} %pad_maximum_fusion, pred[268]{0:T(512)(128)(4,1)S(1)} %fusion.39, pred[332]{0:T(512)(128)(4,1)S(1)} %fusion.38), kind=kLoop, calls=%fused_computation.73 | loop fusion | flops 355904 | bytes 2136024 | tf_op jit(solution)/shard_map/add | solution.py:136
  98.3 1.9 gather_fusion
  100.2 9.1 %scatter_fusion = f32[332,268]{0,1:T(8,128)} fusion(f32[332,268]{0,1:T(8,128)} %get-tuple-element.84, s32[64]{0:T(128)S(1)} %get-tuple-element.110, f32[64]{0:T(128)S(1)} %get-tuple-element.108), kind=kCustom, calls=%fused_computation.3 | custom fusion | flops 64 | bytes 1280 | tf_op jit(solution)/shard_map/scatter-add | solution.py:146
  109.3 2.6 %multiply_bitcast_fusion.2 = (f32[332,268]{0,1:T(8,128)}, f32[1,332,268]{1,2,0:T(8,128)S(1)}, f32[1,332,268]{1,2,0:T(8,128)S(1)}) fusion(f32[1,332,268]{1,2,0:T(8,128)} %divide_add_fusion, f32[1,332,268]{1,2,0:T(8,128)} %get-tuple-element.66, f32[8,332,268]{1,2,0:T(8,128)S(1)} %pad_maximum_fusion, pred[268]{0:T(512)(128)(4,1)S(1)} %fusion.39, ...), kind=kLoop, calls=%fused_computation.67 | loop fusion | flops 1067712 | bytes 3915544 | tf_op jit(solution)/shard_map/reduce_sum | solution.py:168
  113.1 9.1 %scatter_fusion.1 = f32[332,268]{0,1:T(8,128)} fusion(f32[332,268]{0,1:T(8,128)} %fusion.23, s32[64]{0:T(128)S(1)} %get-tuple-element.110, f32[64]{0:T(128)S(1)} %get-tuple-element.107), kind=kCustom, calls=%fused_computation.4 | custom fusion | flops 64 | bytes 1280 | tf_op jit(solution)/shard_map/scatter-add | solution.py:146
  122.2 2.4 %multiply_bitcast_fusion.1 = (f32[332,268]{0,1:T(8,128)}, f32[1,332,268]{1,2,0:T(8,128)S(1)}, f32[1,332,268]{1,2,0:T(8,128)S(1)}) fusion(f32[1,332,268]{1,2,0:T(8,128)} %get-tuple-element.65, f32[8,332,268]{1,2,0:T(8,128)S(1)} %pad_maximum_fusion, pred[268]{0:T(512)(128)(4,1)S(1)} %fusion.39, pred[332]{0:T(512)(128)(4,1)S(1)} %fusion.38, ...), kind=kLoop, calls=%fused_computation.66 | loop fusion | flops 800784 | bytes 3559640 | tf_op jit(solution)/shard_map/reduce_sum | solution.py:168
  125.8 9.1 %scatter_fusion.2 = f32[332,268]{0,1:T(8,128)} fusion(f32[332,268]{0,1:T(8,128)} %fusion.21, s32[64]{0:T(128)S(1)} %get-tuple-element.110, f32[64]{0:T(128)S(1)} %get-tuple-element.62), kind=kCustom, calls=%fused_computation.5 | custom fusion | flops 64 | bytes 1280 | tf_op jit(solution)/shard_map/scatter-add | solution.py:146
  134.9 2.6 %multiply_bitcast_fusion = (f32[332,268]{0,1:T(8,128)S(1)}, f32[1,332,268]{1,2,0:T(8,128)}, f32[1,332,268]{1,2,0:T(8,128)}, f32[1,332,268]{1,2,0:T(8,128)S(1)}) fusion(f32[8,332,268]{1,2,0:T(8,128)S(1)} %pad_maximum_fusion, pred[268]{0:T(512)(128)(4,1)S(1)} %fusion.39, pred[332]{0:T(512)(128)(4,1)S(1)} %fusion.38, f32[1,332,268]{1,2,0:T(8,128)} %copy-done.26, ...), kind=kLoop, calls=%fused_computation.64 | loop fusion | flops 978736 | bytes 4627352 | tf_op jit(solution)/shard_map/reduce_sum | solution.py:168
  137.6 3.3 %fusion.32 = (f32[1,332,268]{1,2,0:T(8,128)S(1)}, f32[1,332,268]{1,2,0:T(8,128)S(1)}, f32[332,268]{0,1:T(8,128)S(1)}, f32[332,268]{0,1:T(8,128)S(1)}, f32[332,268]{0,1:T(8,128)S(1)}, /*index=5*/f32[1,332,268]{1,2,0:T(8,128)S(1)}) fusion(f32[1,332,268]{1,2,0:T(8,128)S(1)} %get-tuple-element.61, f32[1,332,268]{1,2,0:T(8,128)S(1)} %copy-done.32, ...), kind=kLoop, calls=%fused_computation.139 | loop fusion | flops 12723568 | bytes 4626752 | tf_op jit(solution)/shard_map/sub | solution.py:40
  143.0 7.4 %all-gather.3.cloned.1.call-done = f32[4,320,256]{2,1,0:T(8,128)} async-done(((f32[2,320,256]{2,1,0:T(8,128)}), f32[4,320,256]{2,1,0:T(8,128)}) %all-gather.3.cloned.1.call-update) | async-done | bytes 1310736 | tf_op jit(solution)/shard_map/all_gather | solution.py:217
  150.4 1.5 reduce_sum.41
  152.3 3.7 %collective-permute-start.4 = (f32[2,1,256]{1,2,0:T(8,128)S(1)}, f32[2,1,256]{1,2,0:T(8,128)S(1)}, u32[]{:S(2)}, u32[]{:S(2)}) collective-permute-start(f32[2,1,256]{1,2,0:T(8,128)S(1)} %get-tuple-element.97), channel_id=1, source_target_pairs={{0,2},{2,4},{4,6},{1,3},{3,5},{5,7},{8,10},{10,12},{12,14},{9,11},... | collective-permute-start | bytes 6152 | tf_op jit(solution)/shard_map/ppermute | solution.py:18
  156.0 1.6 collective-permute-start.5
  157.6 4.4 %collective-permute-done.4 = f32[2,1,256]{1,2,0:T(8,128)S(1)} collective-permute-done((f32[2,1,256]{1,2,0:T(8,128)S(1)}, f32[2,1,256]{1,2,0:T(8,128)S(1)}, u32[]{:S(2)}, u32[]{:S(2)}) %collective-permute-start.4) | collective-permute-done | bytes 2080 | tf_op jit(solution)/shard_map/ppermute | solution.py:18
  162.0 4.5 %collective-permute-done.5 = f32[2,1,256]{1,2,0:T(8,128)S(1)} collective-permute-done((f32[2,1,256]{1,2,0:T(8,128)S(1)}, f32[2,1,256]{1,2,0:T(8,128)S(1)}, u32[]{:S(2)}, u32[]{:S(2)}) %collective-permute-start.5) | collective-permute-done | bytes 2080 | tf_op jit(solution)/shard_map/ppermute | solution.py:20
  166.5 3.4 %collective-permute-start.6 = (f32[2,322,1]{1,2,0:T(1,128)S(1)}, f32[2,322,1]{1,2,0:T(1,128)S(1)}, u32[]{:S(2)}, u32[]{:S(2)}) collective-permute-start(f32[2,322,1]{1,2,0:T(1,128)S(1)} %get-tuple-element.91), channel_id=1, source_target_pairs={{0,1},{2,3},{4,5},{6,7},{8,9},{10,11},{12,13},{14,15},{16,17},{18,... | collective-permute-start | bytes 7736 | tf_op jit(solution)/shard_map/ppermute | solution.py:18
  171.2 4.2 %collective-permute-done.7 = f32[2,322,1]{1,2,0:T(1,128)S(1)} collective-permute-done((f32[2,322,1]{1,2,0:T(1,128)S(1)}, f32[2,322,1]{1,2,0:T(1,128)S(1)}, u32[]{:S(2)}, u32[]{:S(2)}) %collective-permute-start.7) | collective-permute-done | bytes 2608 | tf_op jit(solution)/shard_map/ppermute | solution.py:20
  176.4 3.4 %collective-permute-start.8 = (f32[2,1,256]{1,2,0:T(8,128)S(1)}, f32[2,1,256]{1,2,0:T(8,128)S(1)}, u32[]{:S(2)}, u32[]{:S(2)}) collective-permute-start(f32[2,1,256]{1,2,0:T(8,128)S(1)} %get-tuple-element.95), channel_id=1, source_target_pairs={{0,2},{2,4},{4,6},{1,3},{3,5},{5,7},{8,10},{10,12},{12,14},{9,11},... | collective-permute-start | bytes 6152 | tf_op jit(solution)/shard_map/ppermute | solution.py:18
  181.1 2.5 %collective-permute-done.8 = f32[2,1,256]{1,2,0:T(8,128)S(1)} collective-permute-done((f32[2,1,256]{1,2,0:T(8,128)S(1)}, f32[2,1,256]{1,2,0:T(8,128)S(1)}, u32[]{:S(2)}, u32[]{:S(2)}) %collective-permute-start.8) | collective-permute-done | bytes 2080 | tf_op jit(solution)/shard_map/ppermute | solution.py:18
  183.6 4.4 %collective-permute-done.9 = f32[2,1,256]{1,2,0:T(8,128)S(1)} collective-permute-done((f32[2,1,256]{1,2,0:T(8,128)S(1)}, f32[2,1,256]{1,2,0:T(8,128)S(1)}, u32[]{:S(2)}, u32[]{:S(2)}) %collective-permute-start.9) | collective-permute-done | bytes 2080 | tf_op jit(solution)/shard_map/ppermute | solution.py:20
  188.1 1.7 collective-permute-start.10
  189.8 1.5 collective-permute-start.11
  191.4 2.4 %slice_subtract_fusion.12 = (f32[1,320,256]{1,2,0:T(8,128)}, f32[1,320,256]{1,2,0:T(8,128)}) fusion(f32[1,332,268]{1,2,0:T(8,128)S(1)} %copy-done.39, f32[1,332,268]{1,2,0:T(8,128)S(1)} %copy-done.38, f32[1,332,268]{1,2,0:T(8,128)S(1)} %get-tuple-element.102, f32[1,332,268]{1,2,0:T(8,128)S(1)} %copy-done.13, f32[1,332,268]{1,2,0:T(8,128)S(1)} %copy-done.25, ...), kind=kLoop, calls=%fused_computation.97 | loop fusion | flops 983040 | bytes 4587520 | tf_op jit(solution)/shard_map/sub | solution.py:170
  193.8 1.9 copy.100
  195.7 1.9 copy.99
  (152 shorter events, 31.7 us)
Async XLA Ops:
  7.2 11.5 %copy-start.43 = (f32[1,320,256]{2,1,0:T(8,128)S(1)}, f32[1,320,256]{2,1,0:T(8,128)}, u32[]{:S(2)}) copy-start(f32[1,320,256]{2,1,0:T(8,128)} %param.32) | copy-start | bytes 983044
  7.2 12.4 %copy-start.44 = (f32[1,320,256]{2,1,0:T(8,128)S(1)}, f32[1,320,256]{2,1,0:T(8,128)}, u32[]{:S(2)}) copy-start(f32[1,320,256]{2,1,0:T(8,128)} %param.33) | copy-start | bytes 983044
  7.2 143.2 %all-gather.3.cloned.1.call-start = ((), (), s32[]{:S(2)}) async-start(), calls=%async_computation | async-start | bytes 1966080 | tf_op jit(solution)/shard_map/all_gather | solution.py:217
  19.8 14.2 %copy-start.42 = (f32[1,320,256]{1,2,0:T(8,128)S(1)}, f32[1,320,256]{1,2,0:T(8,128)}, u32[]{:S(2)}) copy-start(f32[1,320,256]{1,2,0:T(8,128)} %copy.78) | copy-start | bytes 983044
  19.8 14.2 %copy-start.41 = (f32[1,320,256]{1,2,0:T(8,128)S(1)}, f32[1,320,256]{1,2,0:T(8,128)}, u32[]{:S(2)}) copy-start(f32[1,320,256]{1,2,0:T(8,128)} %copy.79) | copy-start | bytes 983044
  19.8 14.2 %copy-start.40 = (f32[1,320,256]{1,2,0:T(8,128)S(1)}, f32[1,320,256]{1,2,0:T(8,128)}, u32[]{:S(2)}) copy-start(f32[1,320,256]{1,2,0:T(8,128)} %copy.80) | copy-start | bytes 983044
  34.1 21.0 %copy-start = (f32[8,320,256]{1,2,0:T(8,128)}, f32[8,320,256]{1,2,0:T(8,128)S(1)}, u32[]{:S(2)}) copy-start(f32[8,320,256]{1,2,0:T(8,128)S(1)} %constant_dynamic-update-slice_fusion) | copy-start | bytes 7864324
  34.1 13.3 %copy-start.45 = (f32[1,3,1]{1,2,0:T(1,128)S(1)}, f32[1,3,1]{1,2,0:T(1,128)}, u32[]{:S(2)}) copy-start(f32[1,3,1]{1,2,0:T(1,128)} %param.26) | copy-start | bytes 40
  34.1 13.9 %copy-start.46 = (s32[64]{0:T(128)S(1)}, s32[64]{0:T(128)}, u32[]{:S(2)}) copy-start(s32[64]{0:T(128)} %param.27) | copy-start | bytes 772
  34.1 13.9 %copy-start.47 = (s32[64]{0:T(128)S(1)}, s32[64]{0:T(128)}, u32[]{:S(2)}) copy-start(s32[64]{0:T(128)} %param.28) | copy-start | bytes 772
  34.2 13.9 %copy-start.49 = (s32[3]{0:T(128)S(1)}, s32[3]{0:T(128)}, u32[]{:S(2)}) copy-start(s32[3]{0:T(128)} %constant.129.clone.1) | copy-start | bytes 40
  37.6 16.2 %collective-permute-start.1 = (f32[8,6,256]{2,0,1:T(8,128)S(1)}, f32[8,6,256]{2,0,1:T(8,128)S(1)}, u32[]{:S(2)}, u32[]{:S(2)}) collective-permute-start(f32[8,6,256]{2,0,1:T(8,128)S(1)} %copy.83), channel_id=1, source_target_pairs={{2,0},{4,2},{6,4},{3,1},{5,3},{7,5},{10,8},{12,10},{14,12},{11,9},... | collective-permute-start | bytes 147464 | tf_op jit(solution)/shard_map/ppermute | solution.py:20
  40.5 12.0 %collective-permute-start = (f32[8,6,256]{2,0,1:T(8,128)S(1)}, f32[8,6,256]{2,0,1:T(8,128)S(1)}, u32[]{:S(2)}, u32[]{:S(2)}) collective-permute-start(f32[8,6,256]{2,0,1:T(8,128)S(1)} %copy.82), channel_id=1, source_target_pairs={{0,2},{2,4},{4,6},{1,3},{3,5},{5,7},{8,10},{10,12},{12,14},{9,11},... | collective-permute-start | bytes 147464 | tf_op jit(solution)/shard_map/ppermute | solution.py:18
  55.1 11.5 %copy-start.16 = (f32[8,6,256]{1,2,0:T(8,128)S(1)}, f32[8,6,256]{1,2,0:T(8,128)}, u32[]{:S(2)}) copy-start(f32[8,6,256]{1,2,0:T(8,128)} %copy.84) | copy-start | bytes 147460
  55.1 11.5 %copy-start.17 = (f32[8,6,256]{1,2,0:T(8,128)S(1)}, f32[8,6,256]{1,2,0:T(8,128)}, u32[]{:S(2)}) copy-start(f32[8,6,256]{1,2,0:T(8,128)} %copy.85) | copy-start | bytes 147460
  56.2 6.0 %collective-permute-start.2 = (f32[8,332,6]{1,2,0:T(8,128)S(1)}, f32[8,332,6]{1,2,0:T(8,128)S(1)}, u32[]{:S(2)}, u32[]{:S(2)}) collective-permute-start(f32[8,332,6]{1,2,0:T(8,128)S(1)} %get-tuple-element.81), channel_id=1, source_target_pairs={{0,1},{2,3},{4,5},{6,7},{8,9},{10,11},{12,13},{14,15},{16,17},{18,... | collective-permute-start | bytes 191240 | tf_op jit(solution)/shard_map/ppermute | solution.py:18
  60.1 6.5 %collective-permute-start.3 = (f32[8,332,6]{1,2,0:T(8,128)S(1)}, f32[8,332,6]{1,2,0:T(8,128)S(1)}, u32[]{:S(2)}, u32[]{:S(2)}) collective-permute-start(f32[8,332,6]{1,2,0:T(8,128)S(1)} %get-tuple-element.82), channel_id=1, source_target_pairs={{1,0},{3,2},{5,4},{7,6},{9,8},{11,10},{13,12},{15,14},{17,16},{19,... | collective-permute-start | bytes 191240 | tf_op jit(solution)/shard_map/ppermute | solution.py:20
  69.9 2.7 %copy-start.31 = (f32[1,332,268]{1,2,0:T(8,128)}, f32[1,332,268]{1,2,0:T(8,128)S(1)}, u32[]{:S(2)}) copy-start(f32[1,332,268]{1,2,0:T(8,128)S(1)} %get-tuple-element.86) | copy-start | bytes 1067716
  89.8 10.4 %copy-start.48 = (f32[1,3,64]{2,0,1:T(1,128)S(1)}, f32[1,3,64]{2,0,1:T(1,128)}, u32[]{:S(2)}) copy-start(f32[1,3,64]{2,0,1:T(1,128)} %param.29) | copy-start | bytes 2308
  109.3 2.6 %copy-start.5 = (f32[1,332,268]{1,2,0:T(8,128)S(1)}, f32[1,332,268]{1,2,0:T(8,128)}, u32[]{:S(2)}) copy-start(f32[1,332,268]{1,2,0:T(8,128)} %get-tuple-element.69) | copy-start | bytes 1067716
  109.3 2.6 %copy-start.8 = (f32[1,332,268]{1,2,0:T(8,128)S(1)}, f32[1,332,268]{1,2,0:T(8,128)}, u32[]{:S(2)}) copy-start(f32[1,332,268]{1,2,0:T(8,128)} %get-tuple-element.70) | copy-start | bytes 1067716
  109.3 2.6 %copy-start.11 = (f32[1,332,268]{1,2,0:T(8,128)S(1)}, f32[1,332,268]{1,2,0:T(8,128)}, u32[]{:S(2)}) copy-start(f32[1,332,268]{1,2,0:T(8,128)} %get-tuple-element.71) | copy-start | bytes 1067716
  109.3 2.6 %copy-start.18 = (f32[332,268]{0,1:T(8,128)S(1)}, f32[332,268]{0,1:T(8,128)}, u32[]{:S(2)}) copy-start(f32[332,268]{0,1:T(8,128)} %scatter_fusion) | copy-start | bytes 1067716
  134.9 2.6 %copy-start.1 = (f32[1,332,268]{1,2,0:T(8,128)S(1)}, f32[1,332,268]{1,2,0:T(8,128)}, u32[]{:S(2)}) copy-start(f32[1,332,268]{1,2,0:T(8,128)} %divide_add_fusion) | copy-start | bytes 1067716
  134.9 2.6 %copy-start.15 = (f32[1,332,268]{1,2,0:T(8,128)S(1)}, f32[1,332,268]{1,2,0:T(8,128)}, u32[]{:S(2)}) copy-start(f32[1,332,268]{1,2,0:T(8,128)} %copy-done.14) | copy-start | bytes 1067716
  134.9 2.6 %copy-start.23 = (f32[332,268]{0,1:T(8,128)S(1)}, f32[332,268]{0,1:T(8,128)}, u32[]{:S(2)}) copy-start(f32[332,268]{0,1:T(8,128)} %copy-done.22) | copy-start | bytes 1067716
  134.9 2.6 %copy-start.28 = (f32[1,332,268]{1,2,0:T(8,128)S(1)}, f32[1,332,268]{1,2,0:T(8,128)}, u32[]{:S(2)}) copy-start(f32[1,332,268]{1,2,0:T(8,128)} %copy-done.27) | copy-start | bytes 1067716
  134.9 2.6 %copy-start.30 = (f32[1,332,268]{1,2,0:T(8,128)S(1)}, f32[1,332,268]{1,2,0:T(8,128)}, u32[]{:S(2)}) copy-start(f32[1,332,268]{1,2,0:T(8,128)} %copy-done.29) | copy-start | bytes 1067716
  134.9 2.6 %copy-start.32 = (f32[1,332,268]{1,2,0:T(8,128)S(1)}, f32[1,332,268]{1,2,0:T(8,128)}, u32[]{:S(2)}) copy-start(f32[1,332,268]{1,2,0:T(8,128)} %copy-done.31) | copy-start | bytes 1067716
  137.5 4.3 %copy-start.24 = (f32[1,332,268]{1,2,0:T(8,128)}, f32[1,332,268]{1,2,0:T(8,128)S(1)}, u32[]{:S(2)}) copy-start(f32[1,332,268]{1,2,0:T(8,128)S(1)} %get-tuple-element.61) | copy-start | bytes 1067716
  137.5 3.4 %copy-start.36 = (f32[332,268]{0,1:T(8,128)S(1)}, f32[332,268]{0,1:T(8,128)}, u32[]{:S(2)}) copy-start(f32[332,268]{0,1:T(8,128)} %get-tuple-element.52) | copy-start | bytes 1067716
  137.5 3.4 %copy-start.37 = (f32[332,268]{0,1:T(8,128)S(1)}, f32[332,268]{0,1:T(8,128)}, u32[]{:S(2)}) copy-start(f32[332,268]{0,1:T(8,128)} %get-tuple-element.55) | copy-start | bytes 1067716
  151.9 29.2 %copy-start.25 = (f32[1,332,268]{1,2,0:T(8,128)S(1)}, f32[1,332,268]{1,2,0:T(8,128)}, u32[]{:S(2)}) copy-start(f32[1,332,268]{1,2,0:T(8,128)} %copy-done.24) | copy-start | bytes 1067716
  152.3 9.7 %collective-permute-start.4 = (f32[2,1,256]{1,2,0:T(8,128)S(1)}, f32[2,1,256]{1,2,0:T(8,128)S(1)}, u32[]{:S(2)}, u32[]{:S(2)}) collective-permute-start(f32[2,1,256]{1,2,0:T(8,128)S(1)} %get-tuple-element.97), channel_id=1, source_target_pairs={{0,2},{2,4},{4,6},{1,3},{3,5},{5,7},{8,10},{10,12},{12,14},{9,11},... | collective-permute-start | bytes 6152 | tf_op jit(solution)/shard_map/ppermute | solution.py:18
  156.0 35.3 %copy-start.4 = (f32[1,332,268]{1,2,0:T(8,128)S(1)}, f32[1,332,268]{1,2,0:T(8,128)}, u32[]{:S(2)}) copy-start(f32[1,332,268]{1,2,0:T(8,128)} %get-tuple-element.68) | copy-start | bytes 1067716
  156.0 35.3 %copy-start.7 = (f32[1,332,268]{1,2,0:T(8,128)S(1)}, f32[1,332,268]{1,2,0:T(8,128)}, u32[]{:S(2)}) copy-start(f32[1,332,268]{1,2,0:T(8,128)} %get-tuple-element.69) | copy-start | bytes 1067716
  156.0 35.3 %copy-start.10 = (f32[1,332,268]{1,2,0:T(8,128)S(1)}, f32[1,332,268]{1,2,0:T(8,128)}, u32[]{:S(2)}) copy-start(f32[1,332,268]{1,2,0:T(8,128)} %get-tuple-element.70) | copy-start | bytes 1067716
  156.0 35.3 %copy-start.13 = (f32[1,332,268]{1,2,0:T(8,128)S(1)}, f32[1,332,268]{1,2,0:T(8,128)}, u32[]{:S(2)}) copy-start(f32[1,332,268]{1,2,0:T(8,128)} %get-tuple-element.71) | copy-start | bytes 1067716
  156.0 35.3 %copy-start.20 = (f32[332,268]{0,1:T(8,128)S(1)}, f32[332,268]{0,1:T(8,128)}, u32[]{:S(2)}) copy-start(f32[332,268]{0,1:T(8,128)} %scatter_fusion.2) | copy-start | bytes 1067716
  156.0 35.3 %copy-start.38 = (f32[1,332,268]{1,2,0:T(8,128)S(1)}, f32[1,332,268]{1,2,0:T(8,128)}, u32[]{:S(2)}) copy-start(f32[1,332,268]{1,2,0:T(8,128)} %get-tuple-element.59) | copy-start | bytes 1067716
  156.0 35.3 %copy-start.39 = (f32[1,332,268]{1,2,0:T(8,128)S(1)}, f32[1,332,268]{1,2,0:T(8,128)}, u32[]{:S(2)}) copy-start(f32[1,332,268]{1,2,0:T(8,128)} %get-tuple-element.60) | copy-start | bytes 1067716
  156.0 10.4 %collective-permute-start.5 = (f32[2,1,256]{1,2,0:T(8,128)S(1)}, f32[2,1,256]{1,2,0:T(8,128)S(1)}, u32[]{:S(2)}, u32[]{:S(2)}) collective-permute-start(f32[2,1,256]{1,2,0:T(8,128)S(1)} %get-tuple-element.98), channel_id=1, source_target_pairs={{2,0},{4,2},{6,4},{3,1},{5,3},{7,5},{10,8},{12,10},{14,12},{11,9},... | collective-permute-start | bytes 6152 | tf_op jit(solution)/shard_map/ppermute | solution.py:20
  166.5 4.7 %collective-permute-start.6 = (f32[2,322,1]{1,2,0:T(1,128)S(1)}, f32[2,322,1]{1,2,0:T(1,128)S(1)}, u32[]{:S(2)}, u32[]{:S(2)}) collective-permute-start(f32[2,322,1]{1,2,0:T(1,128)S(1)} %get-tuple-element.91), channel_id=1, source_target_pairs={{0,1},{2,3},{4,5},{6,7},{8,9},{10,11},{12,13},{14,15},{16,17},{18,... | collective-permute-start | bytes 7736 | tf_op jit(solution)/shard_map/ppermute | solution.py:18
  169.9 5.5 %collective-permute-start.7 = (f32[2,322,1]{1,2,0:T(1,128)S(1)}, f32[2,322,1]{1,2,0:T(1,128)S(1)}, u32[]{:S(2)}, u32[]{:S(2)}) collective-permute-start(f32[2,322,1]{1,2,0:T(1,128)S(1)} %get-tuple-element.92), channel_id=1, source_target_pairs={{1,0},{3,2},{5,4},{7,6},{9,8},{11,10},{13,12},{15,14},{17,16},{19,... | collective-permute-start | bytes 7736 | tf_op jit(solution)/shard_map/ppermute | solution.py:20
  176.4 7.3 %collective-permute-start.8 = (f32[2,1,256]{1,2,0:T(8,128)S(1)}, f32[2,1,256]{1,2,0:T(8,128)S(1)}, u32[]{:S(2)}, u32[]{:S(2)}) collective-permute-start(f32[2,1,256]{1,2,0:T(8,128)S(1)} %get-tuple-element.95), channel_id=1, source_target_pairs={{0,2},{2,4},{4,6},{1,3},{3,5},{5,7},{8,10},{10,12},{12,14},{9,11},... | collective-permute-start | bytes 6152 | tf_op jit(solution)/shard_map/ppermute | solution.py:18
  179.8 8.3 %collective-permute-start.9 = (f32[2,1,256]{1,2,0:T(8,128)S(1)}, f32[2,1,256]{1,2,0:T(8,128)S(1)}, u32[]{:S(2)}, u32[]{:S(2)}) collective-permute-start(f32[2,1,256]{1,2,0:T(8,128)S(1)} %get-tuple-element.96), channel_id=1, source_target_pairs={{2,0},{4,2},{6,4},{3,1},{5,3},{7,5},{10,8},{12,10},{14,12},{11,9},... | collective-permute-start | bytes 6152 | tf_op jit(solution)/shard_map/ppermute | solution.py:20
  188.1 9.4 %collective-permute-start.10 = (f32[2,322,1]{1,2,0:T(1,128)S(1)}, f32[2,322,1]{1,2,0:T(1,128)S(1)}, u32[]{:S(2)}, u32[]{:S(2)}) collective-permute-start(f32[2,322,1]{1,2,0:T(1,128)S(1)} %get-tuple-element.89), channel_id=1, source_target_pairs={{0,1},{2,3},{4,5},{6,7},{8,9},{10,11},{12,13},{14,15},{16,17},{18,... | collective-permute-start | bytes 7736 | tf_op jit(solution)/shard_map/ppermute | solution.py:18
  189.8 7.8 %collective-permute-start.11 = (f32[2,322,1]{1,2,0:T(1,128)S(1)}, f32[2,322,1]{1,2,0:T(1,128)S(1)}, u32[]{:S(2)}, u32[]{:S(2)}) collective-permute-start(f32[2,322,1]{1,2,0:T(1,128)S(1)} %get-tuple-element.90), channel_id=1, source_target_pairs={{1,0},{3,2},{5,4},{7,6},{9,8},{11,10},{13,12},{15,14},{17,16},{19,... | collective-permute-start | bytes 7736 | tf_op jit(solution)/shard_map/ppermute | solution.py:20
  (15 other events, 23.4 us)
Sparse Core Ops, SparseCore 0:
  143.1 7.2 all-gather.2
